TPU v7x, 256 devices: a whole 4x4x8 slice. The times are simulated.
256 devices in a mesh: node: 16 (over z, core), head: 16 (over x, y).
Axes of the slice: x: 4, y: 4, z: 8, core: 2. Of those that a mesh axis runs over, the one named last changes fastest.
Arguments:
- features: bfloat16 [65536, 1024], P(('node', 'head')), may hold values from -6 to 6
- attn_gain: float32 [1024], replicated, may hold values from 0.25 to 1.75
- qkv_weight: bfloat16 [1024, 16, 192], P(None, 'head')
- out_weight: bfloat16 [1024, 1024], replicated, may hold values from -0.1875 to 0.1875
- feedforward_norm_gain: float32 [1024], replicated, may hold values from 0.25 to 1.75
- up_weight: bfloat16 [1024, 2048], replicated, may hold values from -0.1875 to 0.1875
- down_weight: bfloat16 [2048, 1024], replicated, may hold values from -0.125 to 0.125
- tile_pattern: int32 [512, 8], P('node'), may hold values from 0 to 511, as said below
- node_order: int32 [16, 4096], P('node'), may hold values from 0 to 4095, each once within a row
Outputs:
- updated: bfloat16 [65536, 1024], P(('node', 'head'))
Inputs may be any that keep to these rules, and one draw needn't show every extreme that they name: `tile_pattern`: row t names 8 different tiles; the first is t itself; all lie in partitions (tiles p * 32 to (p + 1) * 32 - 1) at cyclic distance at most 2 from t's partition; the second lies 2 partitions below t's and the third 2 above. `node_order`: each row lists every local row of its partition once.
All inputs are finite; a program needn't handle non-finite values.
Results may differ from a plain program's by a relative error of at most 0.0045.
Values may be sent and summed in bfloat16 or wider, within the bound.
A program may use at most 64 MiB of HBM per device.

v0:
```python
import math
import jax
import jax.numpy as jnp
from jax import lax
from jax.sharding import PartitionSpec as P

D = 1024
HD = 64
TILE = 128
NNZ = 8
REACH = 2


def passed_along(x, axis, by):
    size = lax.axis_size(axis)
    return lax.ppermute(x, axis, [(i, (i + by) % size) for i in range(size)])


def layer_norm(values, gain):
    row_mean = jnp.mean(values, -1, keepdims=True)
    centred = values - row_mean
    variance = jnp.mean(centred * centred, -1, keepdims=True)
    return centred * lax.rsqrt(variance + 1e-05) * gain


def shards(
    features,
    attn_gain,
    qkv_weight,
    out_weight,
    feedforward_norm_gain,
    up_weight,
    down_weight,
    tile_pattern,
    node_order,
):
    own_rows = features.shape[0]
    local_heads = qkv_weight.shape[1]
    head_placements = lax.axis_size("head")
    partitions = lax.axis_size("node")
    rows_part = own_rows * head_placements
    query_tiles = rows_part // TILE
    normed = layer_norm(features.astype(jnp.float32), attn_gain).astype(jnp.bfloat16)
    reordered_weight = jnp.concatenate([qkv_weight[:, :, HD:], qkv_weight[:, :, :HD]], -1)
    local_weight = reordered_weight.reshape(D, local_heads * 3 * HD)
    projected = jnp.dot(
        lax.all_gather(normed, "head", axis=0, tiled=True),
        local_weight,
        preferred_element_type=jnp.float32,
    ).astype(jnp.bfloat16)
    projected = projected.reshape(rows_part, local_heads, 3 * HD)
    partition_permutation = node_order[0]
    keyval_rows = projected[:, :, : 2 * HD].reshape(rows_part, local_heads * 2 * HD)
    query_rows = projected[:, :, 2 * HD :].reshape(rows_part, local_heads * HD)
    keyval = jnp.take(keyval_rows, partition_permutation, axis=0)
    queries = jnp.take(query_rows, partition_permutation, axis=0)
    current = passed_along(keyval, "node", -REACH)
    blocks = [current]
    for cycle_step in range(2 * REACH):
        current = passed_along(current, "node", 1)
        blocks.append(current)
    window = jnp.stack(blocks[::-1])
    window_tiles = window.reshape((2 * REACH + 1) * query_tiles, TILE, local_heads * 2 * HD)
    partition = lax.axis_index("node")
    window_position = (
        tile_pattern // query_tiles - partition + REACH + partitions
    ) % partitions * query_tiles + tile_pattern % query_tiles
    tile_group = math.gcd(query_tiles, max(1, 512 // TILE))
    score_scale = 1.0 / math.sqrt(HD)

    def attend(item_pair):
        group_queries, columns = item_pair
        picked = jnp.take(window_tiles, columns.reshape(tile_group * NNZ), axis=0)
        picked = picked.reshape(tile_group, NNZ * TILE, local_heads, 2 * HD)
        key_rows = picked[..., :HD]
        value_rows = picked[..., HD:]
        query_block = group_queries.reshape(tile_group, TILE, local_heads, HD)
        scores = (
            jnp.einsum("gqhd,gmhd->ghqm", query_block, key_rows, preferred_element_type=jnp.float32)
            * score_scale
        )
        row_max = jnp.max(scores, -1, keepdims=True)
        expd = jnp.exp(scores - row_max)
        weight_arrays = (expd / jnp.sum(expd, -1, keepdims=True)).astype(jnp.bfloat16)
        result = jnp.einsum(
            "ghqm,gmhd->gqhd", weight_arrays, value_rows, preferred_element_type=jnp.float32
        ).astype(jnp.bfloat16)
        return result.reshape(tile_group * TILE, local_heads * HD)

    grouped_queries = queries.reshape(
        query_tiles // tile_group, tile_group * TILE, local_heads * HD
    )
    grouped_slots = window_position.reshape(query_tiles // tile_group, tile_group, NNZ)
    attended = lax.map(attend, (grouped_queries, grouped_slots)).reshape(
        rows_part, local_heads * HD
    )
    inverse_order = (
        jnp.zeros((rows_part,), jnp.int32)
        .at[partition_permutation]
        .set(jnp.arange(rows_part, dtype=jnp.int32))
    )
    restored = jnp.take(attended, inverse_order, axis=0)
    gathered_heads = lax.all_to_all(restored, "head", split_axis=0, concat_axis=1, tiled=True)
    residual = features.astype(jnp.float32) + jnp.dot(
        gathered_heads, out_weight, preferred_element_type=jnp.float32
    )
    mlp_input = layer_norm(residual, feedforward_norm_gain).astype(jnp.bfloat16)
    hidden = jax.nn.gelu(jnp.dot(mlp_input, up_weight, preferred_element_type=jnp.float32)).astype(
        jnp.bfloat16
    )
    return (residual + jnp.dot(hidden, down_weight, preferred_element_type=jnp.float32)).astype(
        jnp.bfloat16
    )


def solution(mesh):
    return jax.shard_map(
        shards,
        mesh=mesh,
        in_specs=(
            P(("node", "head"), None),
            P(),
            P(None, "head", None),
            P(),
            P(),
            P(),
            P(),
            P("node", None),
            P("node", None),
        ),
        out_specs=P(("node", "head"), None),
        check_vma=False,
    )
```

profile of v0, /device:TPU:96, one launch (start us, length us, event | category | flops | bytes accessed | tf_op | source)
XLA Modules:
  0.0 371.6 jit_solution(18285803736506806688)
XLA Ops:
  9.3 2.1 fusion.37
  11.5 77.8 %all-gather.2.cloned.1.call-done = bf16[4096,1024]{1,0:T(8,128)(2,1)} async-done(((bf16[256,1024]{1,0:T(8,128)(2,1)}), bf16[4096,1024]{1,0:T(8,128)(2,1)}) %all-gather.2.cloned.1.call-update) | async-done | bytes 8388624 | tf_op jit(solution)/shard_map/all_gather | solution.py:47
  89.3 6.3 %fusion.23 = bf16[4096,1,192]{0,2,1:T(8,128)(2,1)S(1)} fusion(bf16[4096,1024]{1,0:T(8,128)(2,1)} %all-gather.2.cloned.1.call-done, bf16[1024,1,64]{0,2,1:T(8,128)(2,1)S(1)} %slice-done, bf16[1024,1,128]{0,2,1:T(8,128)(2,1)S(1)} %slice-done.1), kind=kOutput, calls=%fused_computation.33 | convolution fusion | flops 1612185600 | bytes 10354688 | tf_op jit(solution)/shard_map/dot_general | solution.py:46
  99.4 15.0 %gather_fusion.1 = bf16[4096,128]{1,0:T(8,128)(2,1)} fusion(bf16[4096,128]{1,0:T(8,128)(2,1)S(1)} %copy.17, s32[4096]{0:T(1024)S(1)} %broadcast_clamp_fusion), kind=kCustom, calls=%fused_computation.3 | custom fusion | bytes 2113536 | tf_op jit(solution)/shard_map/jit(_take)/gather | solution.py:55
  114.4 3.4 broadcast_select_fusion.3
  118.3 25.5 %collective-permute-done = bf16[4096,128]{1,0:T(8,128)(2,1)S(1)} collective-permute-done((bf16[4096,128]{1,0:T(8,128)(2,1)S(1)}, bf16[4096,128]{1,0:T(8,128)(2,1)S(1)}, u32[]{:S(2)}, u32[]{:S(2)}) %collective-permute-start) | collective-permute-done | bytes 1048608 | tf_op jit(solution)/shard_map/ppermute | solution.py:16
  144.8 14.2 %collective-permute-done.1 = bf16[4096,128]{1,0:T(8,128)(2,1)S(1)} collective-permute-done((bf16[4096,128]{1,0:T(8,128)(2,1)S(1)}, bf16[4096,128]{1,0:T(8,128)(2,1)S(1)}, u32[]{:S(2)}, u32[]{:S(2)}) %collective-permute-start.1) | collective-permute-done | bytes 1048608 | tf_op jit(solution)/shard_map/ppermute | solution.py:16
  160.0 14.2 %collective-permute-done.2 = bf16[4096,128]{1,0:T(8,128)(2,1)S(1)} collective-permute-done((bf16[4096,128]{1,0:T(8,128)(2,1)S(1)}, bf16[4096,128]{1,0:T(8,128)(2,1)S(1)}, u32[]{:S(2)}, u32[]{:S(2)}) %collective-permute-start.2) | collective-permute-done | bytes 1048608 | tf_op jit(solution)/shard_map/ppermute | solution.py:16
  174.7 15.7 %scatter_custom_fusion = s32[4096]{0:T(1024)S(1)} fusion(s32[4096]{0:T(1024)S(1)} %bitcast.103, s32[4096]{0:T(1024)S(1)} %iota.3, s32[]{:T(128)} %copy.60), kind=kCustom, calls=%fused_computation.84 | custom fusion | bytes 16388 | tf_op jit(solution)/shard_map/scatter | solution.py:100
  190.5 3.7 collective-permute-start.4
  197.6 15.0 %gather_fusion.2 = bf16[4096,64]{1,0:T(8,128)(2,1)} fusion(bf16[4096,64]{1,0:T(8,128)(2,1)S(1)} %copy.18, s32[4096]{0:T(1024)S(1)} %get-tuple-element.53), kind=kCustom, calls=%fused_computation.clone | custom fusion | bytes 1064960 | tf_op jit(solution)/shard_map/jit(_take)/gather | solution.py:56
  212.6 3.4 broadcast_select_fusion.2
  221.4 2.3 copy-done.3
  223.7 92.5 %while.10 = (s32[]{:T(128)}, bf16[8,512,64]{1,2,0:T(8,128)(2,1)}, s32[8,4,8]{2,1,0:T(4,128)S(1)}, bf16[160,128,128]{2,1,0:T(8,128)(2,1)}, bf16[8,512,64]{1,2,0:T(8,128)(2,1)}, /*index=5*/s32[]{:T(128)}) while((s32[]{:T(128)}, bf16[8,512,64]{1,2,0:T(8,128)(2,1)}, s32[8,4,8]{2,1,0:T(4,128)S(1)}, bf16[160,128,128]{2,1,0:T(8,128)(2,1)}, ...), condition=%wide.region_5.7_spmd, body=%wide.region_2.6_spmd.sunk | while | flops 205557536 | bytes 12936373 | solution.py:94
  224.7 4.2 %gather_fusion = bf16[32,128,128]{2,1,0:T(8,128)(2,1)} fusion(bf16[160,128,128]{2,1,0:T(8,128)(2,1)} %get-tuple-element.105, s32[1024]{0:T(1024)S(1)} %pad_clamp_fusion.2), kind=kCustom, calls=%fused_computation.1.clone.1 | custom fusion | bytes 2097280 | tf_op jit(solution)/shard_map/while/body/eval_jaxpr/jit(_take)/gather | solution.py:73
  231.5 2.0 fusion.86
  236.3 4.2 %gather_fusion = bf16[32,128,128]{2,1,0:T(8,128)(2,1)} fusion(bf16[160,128,128]{2,1,0:T(8,128)(2,1)} %get-tuple-element.105, s32[1024]{0:T(1024)S(1)} %pad_clamp_fusion.2), kind=kCustom, calls=%fused_computation.1.clone.1 | custom fusion | bytes 2097280 | tf_op jit(solution)/shard_map/while/body/eval_jaxpr/jit(_take)/gather | solution.py:73
  243.1 2.0 fusion.86
  247.9 4.2 %gather_fusion = bf16[32,128,128]{2,1,0:T(8,128)(2,1)} fusion(bf16[160,128,128]{2,1,0:T(8,128)(2,1)} %get-tuple-element.105, s32[1024]{0:T(1024)S(1)} %pad_clamp_fusion.2), kind=kCustom, calls=%fused_computation.1.clone.1 | custom fusion | bytes 2097280 | tf_op jit(solution)/shard_map/while/body/eval_jaxpr/jit(_take)/gather | solution.py:73
  254.6 2.0 fusion.86
  259.4 4.2 %gather_fusion = bf16[32,128,128]{2,1,0:T(8,128)(2,1)} fusion(bf16[160,128,128]{2,1,0:T(8,128)(2,1)} %get-tuple-element.105, s32[1024]{0:T(1024)S(1)} %pad_clamp_fusion.2), kind=kCustom, calls=%fused_computation.1.clone.1 | custom fusion | bytes 2097280 | tf_op jit(solution)/shard_map/while/body/eval_jaxpr/jit(_take)/gather | solution.py:73
  266.2 2.0 fusion.86
  271.0 4.2 %gather_fusion = bf16[32,128,128]{2,1,0:T(8,128)(2,1)} fusion(bf16[160,128,128]{2,1,0:T(8,128)(2,1)} %get-tuple-element.105, s32[1024]{0:T(1024)S(1)} %pad_clamp_fusion.2), kind=kCustom, calls=%fused_computation.1.clone.1 | custom fusion | bytes 2097280 | tf_op jit(solution)/shard_map/while/body/eval_jaxpr/jit(_take)/gather | solution.py:73
  282.5 4.2 %gather_fusion = bf16[32,128,128]{2,1,0:T(8,128)(2,1)} fusion(bf16[160,128,128]{2,1,0:T(8,128)(2,1)} %get-tuple-element.105, s32[1024]{0:T(1024)S(1)} %pad_clamp_fusion.2), kind=kCustom, calls=%fused_computation.1.clone.1 | custom fusion | bytes 2097280 | tf_op jit(solution)/shard_map/while/body/eval_jaxpr/jit(_take)/gather | solution.py:73
  294.1 4.2 %gather_fusion = bf16[32,128,128]{2,1,0:T(8,128)(2,1)} fusion(bf16[160,128,128]{2,1,0:T(8,128)(2,1)} %get-tuple-element.105, s32[1024]{0:T(1024)S(1)} %pad_clamp_fusion.2), kind=kCustom, calls=%fused_computation.1.clone.1 | custom fusion | bytes 2097280 | tf_op jit(solution)/shard_map/while/body/eval_jaxpr/jit(_take)/gather | solution.py:73
  300.9 2.0 fusion.86
  305.7 4.2 %gather_fusion = bf16[32,128,128]{2,1,0:T(8,128)(2,1)} fusion(bf16[160,128,128]{2,1,0:T(8,128)(2,1)} %get-tuple-element.105, s32[1024]{0:T(1024)S(1)} %pad_clamp_fusion.2), kind=kCustom, calls=%fused_computation.1.clone.1 | custom fusion | bytes 2097280 | tf_op jit(solution)/shard_map/while/body/eval_jaxpr/jit(_take)/gather | solution.py:73
  312.4 2.0 fusion.86
  317.7 15.0 %gather_fusion.3 = bf16[4096,64]{1,0:T(8,128)(2,1)} fusion(bf16[4096,64]{1,0:T(8,128)(2,1)S(1)} %bitcast.94, s32[4096]{0:T(1024)S(1)} %get-tuple-element.54), kind=kCustom, calls=%fused_computation.2.clone | custom fusion | bytes 1064960 | tf_op jit(solution)/shard_map/jit(_take)/gather | solution.py:102
  332.7 4.3 %broadcast_select_fusion.1 = bf16[4096,64]{1,0:T(8,128)(2,1)} fusion(bf16[4096,64]{1,0:T(8,128)(2,1)} %gather_fusion.3, pred[4096]{0:T(1024)(128)(4,1)S(1)} %compare_and_fusion.1), kind=kLoop, calls=%fused_computation.65 | loop fusion | flops 262144 | bytes 1052672 | tf_op jit(solution)/shard_map/jit(_take)/select_n | solution.py:102
  338.5 16.7 %all_to_all.19 = bf16[16,256,64]{1,2,0:T(8,128)(2,1)S(1)} all-to-all(bf16[16,256,64]{1,2,0:T(8,128)(2,1)S(1)} %copy.21), channel_id=1, replica_groups=mesh['node'=16,'head'=16] {'head'}, dimensions={0} | all-to-all | bytes 1048576 | tf_op jit(solution)/shard_map/all_to_all | solution.py:103
  357.3 7.5 %fusion.32 = bf16[256,1024]{1,0:T(8,128)(2,1)} fusion(f32[256,1024]{1,0:T(8,128)} %copy-done.4, bf16[2048,1024]{1,0:T(8,128)(2,1)} %param.19, bf16[1024,2048]{1,0:T(8,128)(2,1)} %param.18, f32[1024]{0:T(1024)S(1)} %copy-done.14, f32[256]{0:T(256)S(1)} %add_rsqrt_fusion, f32[256]{0:T(256)S(1)} %broadcast_multiply_fusion), kind=kOutput, calls=%fused_computation.47 | convolution fusion | flops 2153775104 | bytes 9967616 | tf_op jit(solution)/shard_map/dot_general | solution.py:111
  (198 shorter events, 70.4 us)
Async XLA Ops:
  6.5 348.7 %copy-start = (bf16[1024,1024]{1,0:T(8,128)(2,1)S(1)}, bf16[1024,1024]{1,0:T(8,128)(2,1)}, u32[]{:S(2)}) copy-start(bf16[1024,1024]{1,0:T(8,128)(2,1)} %param.16) | copy-start | bytes 6291460
  6.5 82.7 %slice-start = ((bf16[1024,1,192]{0,2,1:T(8,128)(2,1)}), bf16[1024,1,64]{0,2,1:T(8,128)(2,1)S(1)}, s32[]{:S(2)}) async-start(bf16[1024,1,192]{0,2,1:T(8,128)(2,1)} %param.15), calls=%async_computation.2 | async-start | bytes 262144 | tf_op jit(solution)/shard_map/slice | solution.py:44
  6.5 82.7 %slice-start.1 = ((bf16[1024,1,192]{0,2,1:T(8,128)(2,1)}), bf16[1024,1,128]{0,2,1:T(8,128)(2,1)S(1)}, s32[]{:S(2)}) async-start(bf16[1024,1,192]{0,2,1:T(8,128)(2,1)} %param.15), calls=%async_computation.3 | async-start | bytes 524288 | tf_op jit(solution)/shard_map/slice | solution.py:44
  6.5 4.9 %copy-start.12 = (s32[1,4096]{1,0:T(1,128)S(1)}, s32[1,4096]{1,0:T(1,128)}, u32[]{:S(2)}) copy-start(s32[1,4096]{1,0:T(1,128)} %param.21) | copy-start | bytes 49156
  6.5 82.7 %all-gather.2.cloned.1.call-start = ((), (), s32[]{:S(2)}) async-start(), calls=%async_computation.1 | async-start | bytes 8912896 | tf_op jit(solution)/shard_map/all_gather | solution.py:47
  95.6 1.1 copy-start.5
  114.4 60.2 %copy-start.13 = (s32[32,8]{0,1:T(8,128)S(1)}, s32[32,8]{0,1:T(8,128)}, u32[]{:S(2)}) copy-start(s32[32,8]{0,1:T(8,128)} %param.20) | copy-start | bytes 3076
  117.8 26.0 %collective-permute-start = (bf16[4096,128]{1,0:T(8,128)(2,1)S(1)}, bf16[4096,128]{1,0:T(8,128)(2,1)S(1)}, u32[]{:S(2)}, u32[]{:S(2)}) collective-permute-start(bf16[4096,128]{1,0:T(8,128)(2,1)S(1)} %broadcast_select_fusion.3), channel_id=1, source_target_pairs={{0,224},{16,240},{32,0},{48,16},{64,32},{80,48},{96,64},{112,80},{... | collective-permute-start | bytes 3145736 | tf_op jit(solution)/shard_map/ppermute | solution.py:16
  143.8 1.0 copy-start.6
  144.8 14.2 %collective-permute-start.1 = (bf16[4096,128]{1,0:T(8,128)(2,1)S(1)}, bf16[4096,128]{1,0:T(8,128)(2,1)S(1)}, u32[]{:S(2)}, u32[]{:S(2)}) collective-permute-start(bf16[4096,128]{1,0:T(8,128)(2,1)S(1)} %collective-permute-done), channel_id=1, source_target_pairs={{0,16},{16,32},{32,48},{48,64},{64,80},{80,96},{96,112},{112,128},... | collective-permute-start | bytes 3145736 | tf_op jit(solution)/shard_map/ppermute | solution.py:16
  159.0 1.0 copy-start.8
  160.0 14.2 %collective-permute-start.2 = (bf16[4096,128]{1,0:T(8,128)(2,1)S(1)}, bf16[4096,128]{1,0:T(8,128)(2,1)S(1)}, u32[]{:S(2)}, u32[]{:S(2)}) collective-permute-start(bf16[4096,128]{1,0:T(8,128)(2,1)S(1)} %collective-permute-done.1), channel_id=1, source_target_pairs={{0,16},{16,32},{32,48},{48,64},{64,80},{80,96},{96,112},{112,128},... | collective-permute-start | bytes 3145736 | tf_op jit(solution)/shard_map/ppermute | solution.py:16
  174.2 20.0 %copy-start.10 = (bf16[4096,128]{1,0:T(8,128)(2,1)}, bf16[4096,128]{1,0:T(8,128)(2,1)S(1)}, u32[]{:S(2)}) copy-start(bf16[4096,128]{1,0:T(8,128)(2,1)S(1)} %collective-permute-done.2) | copy-start | bytes 3145732
  174.2 16.3 %collective-permute-start.3 = (bf16[4096,128]{1,0:T(8,128)(2,1)S(1)}, bf16[4096,128]{1,0:T(8,128)(2,1)}, u32[]{:S(2)}, u32[]{:S(2)}) collective-permute-start(bf16[4096,128]{1,0:T(8,128)(2,1)S(1)} %collective-permute-done.2), channel_id=1, source_target_pairs={{0,16},{16,32},{32,48},{48,64},{64,80},{80,96},{96,112},{112,128},... | collective-permute-start | bytes 3145736 | tf_op jit(solution)/shard_map/ppermute | solution.py:16
  190.5 26.6 %collective-permute-start.4 = (bf16[4096,128]{1,0:T(8,128)(2,1)}, bf16[4096,128]{1,0:T(8,128)(2,1)}, u32[]{:S(2)}, u32[]{:S(2)}) collective-permute-start(bf16[4096,128]{1,0:T(8,128)(2,1)} %collective-permute-done.3), channel_id=1, source_target_pairs={{0,16},{16,32},{32,48},{48,64},{64,80},{80,96},{96,112},{112,128},... | collective-permute-start | bytes 3145736 | tf_op jit(solution)/shard_map/ppermute | solution.py:16
  217.1 2.9 copy-start.11
  218.5 1.6 copy-start.9
  220.0 1.3 copy-start.7
  221.4 2.3 copy-start.3
  231.5 2.0 copy-start.1
  243.1 2.0 copy-start.1
  254.6 2.0 copy-start.1
  266.2 2.0 copy-start.1
  277.8 2.0 copy-start.1
  289.3 2.0 copy-start.1
  300.9 2.0 copy-start.1
  312.4 2.0 copy-start.1
  332.7 22.6 %copy-start.2 = (bf16[256,1024]{1,0:T(8,128)(2,1)S(1)}, bf16[256,1024]{1,0:T(8,128)(2,1)}, u32[]{:S(2)}) copy-start(bf16[256,1024]{1,0:T(8,128)(2,1)} %param.13) | copy-start | bytes 1572868
  355.2 2.1 copy-start.14
  356.1 1.0 copy-start.4
Sparse Core Ops, SparseCore 0:
  11.6 77.6 all-gather.1
where the time goes:
time: 373 us; the launch traced here: 372 us
  local copies, waits for them, and re-layouts  141 us (38%)
  waiting for transfers between devices  132 us (35%)
  matrix products  38.1 us (10%)
  other arithmetic  25.3 us (7%)
  blocking collectives  16.7 us (4%)
  between operations  13.6 us (4%)
  starting transfers between devices  4.69 us (1%)
    all_gather x1, waiting for transfers between devices, shards(): lax.all_gather(normed, 'head', axis=0, tiled=True)  77.8 us
    ppermute x5, waiting for transfers between devices, passed_along(): return lax.ppermute(x, axis, [(i, (i + by) % size) for i in range(size)])  53.9 us
    gather x16, local copies, waits for them, and re-layouts, attend(): picked = jnp.take(window_tiles, columns.reshape(tile_group * NNZ), axis=0)  45.3 us
    all_to_all x1, blocking collectives, shards(): lax.all_to_all(restored, 'head', split_axis=0, concat_axis=1, tiled=True)  16.7 us
    sub x8, matrix products, attend(): expd = jnp.exp(scores - row_max)  15.7 us
    scatter x1, local copies, waits for them, and re-layouts, shards(): inverse_order = jnp.zeros((rows_part,), jnp.int32).at[partition_permutati...  15.7 us
    gather x1, local copies, waits for them, and re-layouts, shards(): keyval = jnp.take(keyval_rows, partition_permutation, axis=0)  15 us
    gather x1, local copies, waits for them, and re-layouts, shards(): restored = jnp.take(attended, inverse_order, axis=0)  15 us
  transfers between devices with their start and end apart: 6, of which 4 were waited for; matrix products, arithmetic and copies ran while one was open for 10% of the time, Pallas kernels for 0%

commit v1 on v0

--- a/solution.py
+++ b/solution.py
@@ -9,6 +9,27 @@
 TILE = 128
 NNZ = 8
 REACH = 2
+
+
+def ring_gather(shard, axis, dim):
+    size, position, rows = (lax.axis_size(axis), lax.axis_index(axis), shard.shape[dim])
+    upward = [(i, (i + 1) % size) for i in range(size)]
+    left = [(i, (i - 1) % size) for i in range(size)]
+    filled = jnp.zeros((*shard.shape[:dim], size * rows, *shard.shape[dim + 1 :]), shard.dtype)
+    filled = lax.dynamic_update_slice_in_dim(filled, shard, position * rows, axis=dim)
+    from_left = from_right = shard
+    halfway = size // 2
+    for step in range(1, halfway + 1):
+        from_left = lax.ppermute(from_left, axis, upward)
+        filled = lax.dynamic_update_slice_in_dim(
+            filled, from_left, (position - step) % size * rows, axis=dim
+        )
+        if step < size - halfway:
+            from_right = lax.ppermute(from_right, axis, left)
+            filled = lax.dynamic_update_slice_in_dim(
+                filled, from_right, (position + step) % size * rows, axis=dim
+            )
+    return filled
 
 
 def passed_along(x, axis, by):
@@ -44,9 +65,7 @@
     reordered_weight = jnp.concatenate([qkv_weight[:, :, HD:], qkv_weight[:, :, :HD]], -1)
     local_weight = reordered_weight.reshape(D, local_heads * 3 * HD)
     projected = jnp.dot(
-        lax.all_gather(normed, "head", axis=0, tiled=True),
-        local_weight,
-        preferred_element_type=jnp.float32,
+        ring_gather(normed, "head", 0), local_weight, preferred_element_type=jnp.float32
     ).astype(jnp.bfloat16)
     projected = projected.reshape(rows_part, local_heads, 3 * HD)
     partition_permutation = node_order[0]

time: 373 us -> 401 us (1.075)
  starting transfers between devices: 4.69 us -> 42.1 us
  waiting for transfers between devices: 132 us -> 106 us
  local copies, waits for them, and re-layouts: 141 us -> 164 us
  between operations: 13.6 us -> 0.66 us
  matrix products: 38.1 us -> 47.6 us
    all_gather x1 -> x0, waiting for transfers between devices: 77.8 us -> none  [shards(): lax.all_gather(normed, 'head', axis=0, tiled=True)]
    ppermute x0 -> x15, waiting for transfers between devices: none -> 59 us  [the longest x8 59 us: ring_gather(): from_left = lax.ppermute(from_left, axis, upward)]
    ppermute x0 -> x15, starting transfers between devices: none -> 37.6 us  [the longest x7 35.9 us: ring_gather(): from_right = lax.ppermute(from_right, axis, left)]
    dynamic_update_slice x0 -> x15, local copies, waits for them, and re-layouts: none -> 19.8 us  [the longest x7 9.97 us: ring_gather(): lax.dynamic_update_slice_in_dim(filled, from_right, (position + step) % s...]
    dot_general x8, matrix products: 7.85 us -> 17.5 us  [attend(): jnp.einsum('ghqm,gmhd->gqhd', weight_arrays, value_rows, preferred_elemen...]
    ppermute x5, waiting for transfers between devices: 53.9 us -> 47.3 us  [passed_along(): return lax.ppermute(x, axis, [(i, (i + by) % size) for i in range(size)])]
    unnamed x32 -> x46, local copies, waits for them, and re-layouts: 10.4 us -> 13.1 us
  transfers between devices with their start and end apart: 6 -> 20, of which waited for: 4 -> 11; matrix products, arithmetic and copies ran while one was open for 10% -> 14% of each run, Pallas kernels for 0% -> 0%
where the time goes in v1:
time: 401 us; the launch traced here: 398 us
  local copies, waits for them, and re-layouts  164 us (41%)
  waiting for transfers between devices  106 us (26%)
  matrix products  47.6 us (12%)
  starting transfers between devices  42.1 us (10%)
  other arithmetic  22.3 us (6%)
  blocking collectives  15.5 us (4%)
    ppermute x8, waiting for transfers between devices, ring_gather(): from_left = lax.ppermute(from_left, axis, upward)  59 us
    ppermute x5, waiting for transfers between devices, passed_along(): return lax.ppermute(x, axis, [(i, (i + by) % size) for i in range(size)])  47.3 us
    gather x16, local copies, waits for them, and re-layouts, attend(): picked = jnp.take(window_tiles, columns.reshape(tile_group * NNZ), axis=0)  45 us
    ppermute x7, starting transfers between devices, ring_gather(): from_right = lax.ppermute(from_right, axis, left)  35.9 us
    dot_general x8, matrix products, attend(): jnp.einsum('ghqm,gmhd->gqhd', weight_arrays, value_rows, preferred_elemen...  17.5 us
    scatter x1, local copies, waits for them, and re-layouts, shards(): inverse_order = jnp.zeros((rows_part,), jnp.int32).at[partition_permutati...  15.7 us
    all_to_all x1, blocking collectives, shards(): lax.all_to_all(restored, 'head', split_axis=0, concat_axis=1, tiled=True)  15.5 us
    sub x8, matrix products, attend(): expd = jnp.exp(scores - row_max)  15.1 us
  transfers between devices with their start and end apart: 20, of which 11 were waited for; matrix products, arithmetic and copies ran while one was open for 14% of the time, Pallas kernels for 0%

profile of v1, /device:TPU:96, one launch (start us, length us, event | category | flops | bytes accessed | tf_op | source)
XLA Modules:
  0.0 398.4 jit_solution(15056035523091115217)
XLA Ops:
  9.0 3.8 collective-permute-start.1
  12.7 11.8 %collective-permute-done = bf16[256,1024]{1,0:T(8,128)(2,1)S(1)} collective-permute-done((bf16[256,1024]{1,0:T(8,128)(2,1)S(1)}, bf16[256,1024]{1,0:T(8,128)(2,1)S(1)}, u32[]{:S(2)}, u32[]{:S(2)}) %collective-permute-start) | collective-permute-done | bytes 524320 | tf_op jit(solution)/shard_map/ppermute | solution.py:23
  24.5 5.3 %collective-permute-start.3 = (bf16[256,1024]{1,0:T(8,128)(2,1)S(1)}, bf16[256,1024]{1,0:T(8,128)(2,1)S(1)}, u32[]{:S(2)}, u32[]{:S(2)}) collective-permute-start(bf16[256,1024]{1,0:T(8,128)(2,1)S(1)} %collective-permute-done.1), channel_id=1, source_target_pairs={{0,15},{1,0},{2,1},{3,2},{4,3},{5,4},{6,5},{7,6},{8,7},{9,8},{10,9... | collective-permute-start | bytes 1572872 | tf_op jit(solution)/shard_map/ppermute | solution.py:28
  29.9 10.9 %collective-permute-done.2 = bf16[256,1024]{1,0:T(8,128)(2,1)S(1)} collective-permute-done((bf16[256,1024]{1,0:T(8,128)(2,1)S(1)}, bf16[256,1024]{1,0:T(8,128)(2,1)S(1)}, u32[]{:S(2)}, u32[]{:S(2)}) %collective-permute-start.2) | collective-permute-done | bytes 524320 | tf_op jit(solution)/shard_map/ppermute | solution.py:23
  40.8 5.3 %collective-permute-start.5 = (bf16[256,1024]{1,0:T(8,128)(2,1)S(1)}, bf16[256,1024]{1,0:T(8,128)(2,1)S(1)}, u32[]{:S(2)}, u32[]{:S(2)}) collective-permute-start(bf16[256,1024]{1,0:T(8,128)(2,1)S(1)} %collective-permute-done.3), channel_id=1, source_target_pairs={{0,15},{1,0},{2,1},{3,2},{4,3},{5,4},{6,5},{7,6},{8,7},{9,8},{10,9... | collective-permute-start | bytes 1572872 | tf_op jit(solution)/shard_map/ppermute | solution.py:28
  46.2 10.1 %collective-permute-done.4 = bf16[256,1024]{1,0:T(8,128)(2,1)S(1)} collective-permute-done((bf16[256,1024]{1,0:T(8,128)(2,1)S(1)}, bf16[256,1024]{1,0:T(8,128)(2,1)S(1)}, u32[]{:S(2)}, u32[]{:S(2)}) %collective-permute-start.4) | collective-permute-done | bytes 524320 | tf_op jit(solution)/shard_map/ppermute | solution.py:23
  56.2 5.3 %collective-permute-start.7 = (bf16[256,1024]{1,0:T(8,128)(2,1)S(1)}, bf16[256,1024]{1,0:T(8,128)(2,1)}, u32[]{:S(2)}, u32[]{:S(2)}) collective-permute-start(bf16[256,1024]{1,0:T(8,128)(2,1)S(1)} %collective-permute-done.5), channel_id=1, source_target_pairs={{0,15},{1,0},{2,1},{3,2},{4,3},{5,4},{6,5},{7,6},{8,7},{9,8},{10,9... | collective-permute-start | bytes 1572872 | tf_op jit(solution)/shard_map/ppermute | solution.py:28
  61.6 9.2 %collective-permute-done.6 = bf16[256,1024]{1,0:T(8,128)(2,1)S(1)} collective-permute-done((bf16[256,1024]{1,0:T(8,128)(2,1)S(1)}, bf16[256,1024]{1,0:T(8,128)(2,1)S(1)}, u32[]{:S(2)}, u32[]{:S(2)}) %collective-permute-start.6) | collective-permute-done | bytes 524320 | tf_op jit(solution)/shard_map/ppermute | solution.py:23
  71.0 5.4 %collective-permute-start.9 = (bf16[256,1024]{1,0:T(8,128)(2,1)}, bf16[256,1024]{1,0:T(8,128)(2,1)}, u32[]{:S(2)}, u32[]{:S(2)}) collective-permute-start(bf16[256,1024]{1,0:T(8,128)(2,1)} %collective-permute-done.7), channel_id=1, source_target_pairs={{0,15},{1,0},{2,1},{3,2},{4,3},{5,4},{6,5},{7,6},{8,7},{9,8},{10,9... | collective-permute-start | bytes 1572872 | tf_op jit(solution)/shard_map/ppermute | solution.py:28
  76.4 8.3 %collective-permute-done.8 = bf16[256,1024]{1,0:T(8,128)(2,1)} collective-permute-done((bf16[256,1024]{1,0:T(8,128)(2,1)S(1)}, bf16[256,1024]{1,0:T(8,128)(2,1)}, u32[]{:S(2)}, u32[]{:S(2)}) %collective-permute-start.8) | collective-permute-done | bytes 524320 | tf_op jit(solution)/shard_map/ppermute | solution.py:23
  89.6 5.3 %collective-permute-start.11 = (bf16[256,1024]{1,0:T(8,128)(2,1)}, bf16[256,1024]{1,0:T(8,128)(2,1)S(1)}, u32[]{:S(2)}, u32[]{:S(2)}) collective-permute-start(bf16[256,1024]{1,0:T(8,128)(2,1)} %collective-permute-done.9), channel_id=1, source_target_pairs={{0,15},{1,0},{2,1},{3,2},{4,3},{5,4},{6,5},{7,6},{8,7},{9,8},{10,9... | collective-permute-start | bytes 1572872 | tf_op jit(solution)/shard_map/ppermute | solution.py:28
  102.2 5.5 %collective-permute-start.13 = (bf16[256,1024]{1,0:T(8,128)(2,1)S(1)}, bf16[256,1024]{1,0:T(8,128)(2,1)S(1)}, u32[]{:S(2)}, u32[]{:S(2)}) collective-permute-start(bf16[256,1024]{1,0:T(8,128)(2,1)S(1)} %collective-permute-done.11), channel_id=1, source_target_pairs={{0,15},{1,0},{2,1},{3,2},{4,3},{5,4},{6,5},{7,6},{8,7},{9,8},{10,9... | collective-permute-start | bytes 1572872 | tf_op jit(solution)/shard_map/ppermute | solution.py:28
  117.2 6.3 %collective-permute-done.14 = bf16[256,1024]{1,0:T(8,128)(2,1)S(1)} collective-permute-done((bf16[256,1024]{1,0:T(8,128)(2,1)S(1)}, bf16[256,1024]{1,0:T(8,128)(2,1)S(1)}, u32[]{:S(2)}, u32[]{:S(2)}) %collective-permute-start.14) | collective-permute-done | bytes 524320 | tf_op jit(solution)/shard_map/ppermute | solution.py:23
  124.3 6.3 %fusion.23 = bf16[4096,1,192]{0,2,1:T(8,128)(2,1)S(1)} fusion(bf16[4096,1024]{1,0:T(8,128)(2,1)} %constant_dynamic-update-slice_fusion.1, bf16[1024,1,64]{0,2,1:T(8,128)(2,1)S(1)} %slice-done.1, bf16[1024,1,128]{0,2,1:T(8,128)(2,1)S(1)} %slice-done), kind=kOutput, calls=%fused_computation.33 | convolution fusion | flops 1612185600 | bytes 10354688 | tf_op jit(solution)/shard_map/dot_general | solution.py:67
  134.4 14.9 %gather_fusion.1 = bf16[4096,128]{1,0:T(8,128)(2,1)} fusion(bf16[4096,128]{1,0:T(8,128)(2,1)S(1)} %copy.17, s32[4096]{0:T(1024)S(1)} %broadcast_clamp_fusion), kind=kCustom, calls=%fused_computation.3 | custom fusion | bytes 2113536 | tf_op jit(solution)/shard_map/jit(_take)/gather | solution.py:74
  152.9 18.9 %collective-permute-done.15 = bf16[4096,128]{1,0:T(8,128)(2,1)S(1)} collective-permute-done((bf16[4096,128]{1,0:T(8,128)(2,1)S(1)}, bf16[4096,128]{1,0:T(8,128)(2,1)S(1)}, u32[]{:S(2)}, u32[]{:S(2)}) %collective-permute-start.15) | collective-permute-done | bytes 1048608 | tf_op jit(solution)/shard_map/ppermute | solution.py:37
  172.8 14.2 %collective-permute-done.16 = bf16[4096,128]{1,0:T(8,128)(2,1)S(1)} collective-permute-done((bf16[4096,128]{1,0:T(8,128)(2,1)S(1)}, bf16[4096,128]{1,0:T(8,128)(2,1)S(1)}, u32[]{:S(2)}, u32[]{:S(2)}) %collective-permute-start.16) | collective-permute-done | bytes 1048608 | tf_op jit(solution)/shard_map/ppermute | solution.py:37
  188.0 14.2 %collective-permute-done.17 = bf16[4096,128]{1,0:T(8,128)(2,1)S(1)} collective-permute-done((bf16[4096,128]{1,0:T(8,128)(2,1)S(1)}, bf16[4096,128]{1,0:T(8,128)(2,1)S(1)}, u32[]{:S(2)}, u32[]{:S(2)}) %collective-permute-start.17) | collective-permute-done | bytes 1048608 | tf_op jit(solution)/shard_map/ppermute | solution.py:37
  202.8 15.7 %scatter_custom_fusion = s32[4096]{0:T(1024)S(1)} fusion(s32[4096]{0:T(1024)S(1)} %bitcast.102, s32[4096]{0:T(1024)S(1)} %iota.3, s32[]{:T(128)} %copy.76), kind=kCustom, calls=%fused_computation.84 | custom fusion | bytes 16388 | tf_op jit(solution)/shard_map/scatter | solution.py:119
  225.8 14.9 %gather_fusion.2 = bf16[4096,64]{1,0:T(8,128)(2,1)} fusion(bf16[4096,64]{1,0:T(8,128)(2,1)S(1)} %copy.18, s32[4096]{0:T(1024)S(1)} %get-tuple-element.55), kind=kCustom, calls=%fused_computation.clone | custom fusion | bytes 1064960 | tf_op jit(solution)/shard_map/jit(_take)/gather | solution.py:75
  252.1 100.8 %while.10 = (s32[]{:T(128)}, bf16[8,512,64]{1,2,0:T(8,128)(2,1)}, s32[8,4,8]{2,1,0:T(4,128)S(1)}, bf16[160,128,128]{2,1,0:T(8,128)(2,1)}, bf16[8,512,64]{1,2,0:T(8,128)(2,1)}, /*index=5*/s32[]{:T(128)}) while((s32[]{:T(128)}, bf16[8,512,64]{1,2,0:T(8,128)(2,1)}, s32[8,4,8]{2,1,0:T(4,128)S(1)}, bf16[160,128,128]{2,1,0:T(8,128)(2,1)}, ...), condition=%wide.region_5.7_spmd, body=%wide.region_2.0_spmd.sunk | while | flops 205557536 | bytes 8742541 | solution.py:113
  252.2 4.1 %gather_fusion = bf16[32,128,128]{2,1,0:T(8,128)(2,1)} fusion(bf16[160,128,128]{2,1,0:T(8,128)(2,1)} %get-tuple-element.107, s32[1024]{0:T(1024)S(1)} %pad_clamp_fusion.2), kind=kCustom, calls=%fused_computation.1.clone.1 | custom fusion | bytes 2097280 | tf_op jit(solution)/shard_map/while/body/eval_jaxpr/jit(_take)/gather | solution.py:92
  264.8 4.1 %gather_fusion = bf16[32,128,128]{2,1,0:T(8,128)(2,1)} fusion(bf16[160,128,128]{2,1,0:T(8,128)(2,1)} %get-tuple-element.107, s32[1024]{0:T(1024)S(1)} %pad_clamp_fusion.2), kind=kCustom, calls=%fused_computation.1.clone.1 | custom fusion | bytes 2097280 | tf_op jit(solution)/shard_map/while/body/eval_jaxpr/jit(_take)/gather | solution.py:92
  277.4 4.1 %gather_fusion = bf16[32,128,128]{2,1,0:T(8,128)(2,1)} fusion(bf16[160,128,128]{2,1,0:T(8,128)(2,1)} %get-tuple-element.107, s32[1024]{0:T(1024)S(1)} %pad_clamp_fusion.2), kind=kCustom, calls=%fused_computation.1.clone.1 | custom fusion | bytes 2097280 | tf_op jit(solution)/shard_map/while/body/eval_jaxpr/jit(_take)/gather | solution.py:92
  289.9 4.1 %gather_fusion = bf16[32,128,128]{2,1,0:T(8,128)(2,1)} fusion(bf16[160,128,128]{2,1,0:T(8,128)(2,1)} %get-tuple-element.107, s32[1024]{0:T(1024)S(1)} %pad_clamp_fusion.2), kind=kCustom, calls=%fused_computation.1.clone.1 | custom fusion | bytes 2097280 | tf_op jit(solution)/shard_map/while/body/eval_jaxpr/jit(_take)/gather | solution.py:92
  302.5 4.1 %gather_fusion = bf16[32,128,128]{2,1,0:T(8,128)(2,1)} fusion(bf16[160,128,128]{2,1,0:T(8,128)(2,1)} %get-tuple-element.107, s32[1024]{0:T(1024)S(1)} %pad_clamp_fusion.2), kind=kCustom, calls=%fused_computation.1.clone.1 | custom fusion | bytes 2097280 | tf_op jit(solution)/shard_map/while/body/eval_jaxpr/jit(_take)/gather | solution.py:92
  315.1 4.1 %gather_fusion = bf16[32,128,128]{2,1,0:T(8,128)(2,1)} fusion(bf16[160,128,128]{2,1,0:T(8,128)(2,1)} %get-tuple-element.107, s32[1024]{0:T(1024)S(1)} %pad_clamp_fusion.2), kind=kCustom, calls=%fused_computation.1.clone.1 | custom fusion | bytes 2097280 | tf_op jit(solution)/shard_map/while/body/eval_jaxpr/jit(_take)/gather | solution.py:92
  327.7 4.1 %gather_fusion = bf16[32,128,128]{2,1,0:T(8,128)(2,1)} fusion(bf16[160,128,128]{2,1,0:T(8,128)(2,1)} %get-tuple-element.107, s32[1024]{0:T(1024)S(1)} %pad_clamp_fusion.2), kind=kCustom, calls=%fused_computation.1.clone.1 | custom fusion | bytes 2097280 | tf_op jit(solution)/shard_map/while/body/eval_jaxpr/jit(_take)/gather | solution.py:92
  340.3 4.1 %gather_fusion = bf16[32,128,128]{2,1,0:T(8,128)(2,1)} fusion(bf16[160,128,128]{2,1,0:T(8,128)(2,1)} %get-tuple-element.107, s32[1024]{0:T(1024)S(1)} %pad_clamp_fusion.2), kind=kCustom, calls=%fused_computation.1.clone.1 | custom fusion | bytes 2097280 | tf_op jit(solution)/shard_map/while/body/eval_jaxpr/jit(_take)/gather | solution.py:92
  354.3 14.9 %gather_fusion.3 = bf16[4096,64]{1,0:T(8,128)(2,1)} fusion(bf16[4096,64]{1,0:T(8,128)(2,1)S(1)} %bitcast.93, s32[4096]{0:T(1024)S(1)} %get-tuple-element.56), kind=kCustom, calls=%fused_computation.2.clone | custom fusion | bytes 1064960 | tf_op jit(solution)/shard_map/jit(_take)/gather | solution.py:121
  373.8 15.5 %all_to_all.19 = bf16[16,256,64]{1,2,0:T(8,128)(2,1)S(1)} all-to-all(bf16[16,256,64]{1,2,0:T(8,128)(2,1)} %copy.21), channel_id=1, replica_groups=mesh['node'=16,'head'=16] {'head'}, dimensions={0} | all-to-all | bytes 1048576 | tf_op jit(solution)/shard_map/all_to_all | solution.py:122
  391.4 6.9 %fusion.32 = bf16[256,1024]{1,0:T(8,128)(2,1)} fusion(f32[256,1024]{1,0:T(8,128)S(1)} %get-tuple-element.54, bf16[2048,1024]{1,0:T(8,128)(2,1)} %param.19, bf16[1024,2048]{1,0:T(8,128)(2,1)} %param.18, f32[1024]{0:T(1024)S(1)} %copy-done.20, f32[256]{0:T(256)S(1)} %add_rsqrt_fusion, f32[256]{0:T(256)S(1)} %broadcast_multiply_fusion), kind=kOutput, calls=%fused_computation.47 | convolution fusion | flops 2153775104 | bytes 9967616 | tf_op jit(solution)/shard_map/dot_general | solution.py:130
  (239 shorter events, 135.3 us)
Async XLA Ops:
  0.0 389.3 %copy-start = (bf16[1024,1024]{1,0:T(8,128)(2,1)S(1)}, bf16[1024,1024]{1,0:T(8,128)(2,1)}, u32[]{:S(2)}) copy-start(bf16[1024,1024]{1,0:T(8,128)(2,1)} %param.16) | copy-start | bytes 6291460
  1.4 69.5 %copy-start.17 = (s32[1,4096]{1,0:T(1,128)S(1)}, s32[1,4096]{1,0:T(1,128)}, u32[]{:S(2)}) copy-start(s32[1,4096]{1,0:T(1,128)} %param.21) | copy-start | bytes 49156
  7.4 17.1 %collective-permute-start = (bf16[256,1024]{1,0:T(8,128)(2,1)S(1)}, bf16[256,1024]{1,0:T(8,128)(2,1)S(1)}, u32[]{:S(2)}, u32[]{:S(2)}) collective-permute-start(bf16[256,1024]{1,0:T(8,128)(2,1)S(1)} %get-tuple-element.52), channel_id=1, source_target_pairs={{0,1},{1,2},{2,3},{3,4},{4,5},{5,6},{6,7},{7,8},{8,9},{9,10},{10,1... | collective-permute-start | bytes 1572872 | tf_op jit(solution)/shard_map/ppermute | solution.py:23
  9.0 15.6 %collective-permute-start.1 = (bf16[256,1024]{1,0:T(8,128)(2,1)S(1)}, bf16[256,1024]{1,0:T(8,128)(2,1)S(1)}, u32[]{:S(2)}, u32[]{:S(2)}) collective-permute-start(bf16[256,1024]{1,0:T(8,128)(2,1)S(1)} %get-tuple-element.52), channel_id=1, source_target_pairs={{0,15},{1,0},{2,1},{3,2},{4,3},{5,4},{6,5},{7,6},{8,7},{9,8},{10,9... | collective-permute-start | bytes 1572872 | tf_op jit(solution)/shard_map/ppermute | solution.py:28
  24.5 16.3 %collective-permute-start.2 = (bf16[256,1024]{1,0:T(8,128)(2,1)S(1)}, bf16[256,1024]{1,0:T(8,128)(2,1)S(1)}, u32[]{:S(2)}, u32[]{:S(2)}) collective-permute-start(bf16[256,1024]{1,0:T(8,128)(2,1)S(1)} %collective-permute-done), channel_id=1, source_target_pairs={{0,1},{1,2},{2,3},{3,4},{4,5},{5,6},{6,7},{7,8},{8,9},{9,10},{10,1... | collective-permute-start | bytes 1572872 | tf_op jit(solution)/shard_map/ppermute | solution.py:23
  24.5 46.4 %copy-start.12 = (bf16[256,1024]{1,0:T(8,128)(2,1)}, bf16[256,1024]{1,0:T(8,128)(2,1)S(1)}, u32[]{:S(2)}) copy-start(bf16[256,1024]{1,0:T(8,128)(2,1)S(1)} %collective-permute-done.1) | copy-start | bytes 1572868
  24.5 16.3 %collective-permute-start.3 = (bf16[256,1024]{1,0:T(8,128)(2,1)S(1)}, bf16[256,1024]{1,0:T(8,128)(2,1)S(1)}, u32[]{:S(2)}, u32[]{:S(2)}) collective-permute-start(bf16[256,1024]{1,0:T(8,128)(2,1)S(1)} %collective-permute-done.1), channel_id=1, source_target_pairs={{0,15},{1,0},{2,1},{3,2},{4,3},{5,4},{6,5},{7,6},{8,7},{9,8},{10,9... | collective-permute-start | bytes 1572872 | tf_op jit(solution)/shard_map/ppermute | solution.py:28
  40.8 30.0 %copy-start.16 = (bf16[256,1024]{1,0:T(8,128)(2,1)}, bf16[256,1024]{1,0:T(8,128)(2,1)S(1)}, u32[]{:S(2)}) copy-start(bf16[256,1024]{1,0:T(8,128)(2,1)S(1)} %collective-permute-done.2) | copy-start | bytes 1572868
  40.8 15.4 %collective-permute-start.4 = (bf16[256,1024]{1,0:T(8,128)(2,1)S(1)}, bf16[256,1024]{1,0:T(8,128)(2,1)S(1)}, u32[]{:S(2)}, u32[]{:S(2)}) collective-permute-start(bf16[256,1024]{1,0:T(8,128)(2,1)S(1)} %collective-permute-done.2), channel_id=1, source_target_pairs={{0,1},{1,2},{2,3},{3,4},{4,5},{5,6},{6,7},{7,8},{8,9},{9,10},{10,1... | collective-permute-start | bytes 1572872 | tf_op jit(solution)/shard_map/ppermute | solution.py:23
  40.8 30.0 %copy-start.13 = (bf16[256,1024]{1,0:T(8,128)(2,1)}, bf16[256,1024]{1,0:T(8,128)(2,1)S(1)}, u32[]{:S(2)}) copy-start(bf16[256,1024]{1,0:T(8,128)(2,1)S(1)} %collective-permute-done.3) | copy-start | bytes 1572868
  40.8 15.4 %collective-permute-start.5 = (bf16[256,1024]{1,0:T(8,128)(2,1)S(1)}, bf16[256,1024]{1,0:T(8,128)(2,1)S(1)}, u32[]{:S(2)}, u32[]{:S(2)}) collective-permute-start(bf16[256,1024]{1,0:T(8,128)(2,1)S(1)} %collective-permute-done.3), channel_id=1, source_target_pairs={{0,15},{1,0},{2,1},{3,2},{4,3},{5,4},{6,5},{7,6},{8,7},{9,8},{10,9... | collective-permute-start | bytes 1572872 | tf_op jit(solution)/shard_map/ppermute | solution.py:28
  56.2 14.6 %collective-permute-start.6 = (bf16[256,1024]{1,0:T(8,128)(2,1)S(1)}, bf16[256,1024]{1,0:T(8,128)(2,1)S(1)}, u32[]{:S(2)}, u32[]{:S(2)}) collective-permute-start(bf16[256,1024]{1,0:T(8,128)(2,1)S(1)} %collective-permute-done.4), channel_id=1, source_target_pairs={{0,1},{1,2},{2,3},{3,4},{4,5},{5,6},{6,7},{7,8},{8,9},{9,10},{10,1... | collective-permute-start | bytes 1572872 | tf_op jit(solution)/shard_map/ppermute | solution.py:23
  56.2 14.6 %copy-start.10 = (bf16[256,1024]{1,0:T(8,128)(2,1)}, bf16[256,1024]{1,0:T(8,128)(2,1)S(1)}, u32[]{:S(2)}) copy-start(bf16[256,1024]{1,0:T(8,128)(2,1)S(1)} %collective-permute-done.5) | copy-start | bytes 1572868
  56.2 14.7 %collective-permute-start.7 = (bf16[256,1024]{1,0:T(8,128)(2,1)S(1)}, bf16[256,1024]{1,0:T(8,128)(2,1)}, u32[]{:S(2)}, u32[]{:S(2)}) collective-permute-start(bf16[256,1024]{1,0:T(8,128)(2,1)S(1)} %collective-permute-done.5), channel_id=1, source_target_pairs={{0,15},{1,0},{2,1},{3,2},{4,3},{5,4},{6,5},{7,6},{8,7},{9,8},{10,9... | collective-permute-start | bytes 1572872 | tf_op jit(solution)/shard_map/ppermute | solution.py:28
  70.8 13.9 %collective-permute-start.8 = (bf16[256,1024]{1,0:T(8,128)(2,1)S(1)}, bf16[256,1024]{1,0:T(8,128)(2,1)}, u32[]{:S(2)}, u32[]{:S(2)}) collective-permute-start(bf16[256,1024]{1,0:T(8,128)(2,1)S(1)} %collective-permute-done.6), channel_id=1, source_target_pairs={{0,1},{1,2},{2,3},{3,4},{4,5},{5,6},{6,7},{7,8},{8,9},{9,10},{10,1... | collective-permute-start | bytes 1572872 | tf_op jit(solution)/shard_map/ppermute | solution.py:23
  71.0 18.7 %collective-permute-start.9 = (bf16[256,1024]{1,0:T(8,128)(2,1)}, bf16[256,1024]{1,0:T(8,128)(2,1)}, u32[]{:S(2)}, u32[]{:S(2)}) collective-permute-start(bf16[256,1024]{1,0:T(8,128)(2,1)} %collective-permute-done.7), channel_id=1, source_target_pairs={{0,15},{1,0},{2,1},{3,2},{4,3},{5,4},{6,5},{7,6},{8,7},{9,8},{10,9... | collective-permute-start | bytes 1572872 | tf_op jit(solution)/shard_map/ppermute | solution.py:28
  84.7 13.2 %collective-permute-start.10 = (bf16[256,1024]{1,0:T(8,128)(2,1)}, bf16[256,1024]{1,0:T(8,128)(2,1)}, u32[]{:S(2)}, u32[]{:S(2)}) collective-permute-start(bf16[256,1024]{1,0:T(8,128)(2,1)} %collective-permute-done.8), channel_id=1, source_target_pairs={{0,1},{1,2},{2,3},{3,4},{4,5},{5,6},{6,7},{7,8},{8,9},{9,10},{10,1... | collective-permute-start | bytes 1572872 | tf_op jit(solution)/shard_map/ppermute | solution.py:23
  85.0 14.5 %copy-start.15 = (bf16[256,1024]{1,0:T(8,128)(2,1)S(1)}, bf16[256,1024]{1,0:T(8,128)(2,1)}, u32[]{:S(2)}) copy-start(bf16[256,1024]{1,0:T(8,128)(2,1)} %copy-done.14) | copy-start | bytes 1572868
  89.6 12.6 %collective-permute-start.11 = (bf16[256,1024]{1,0:T(8,128)(2,1)}, bf16[256,1024]{1,0:T(8,128)(2,1)S(1)}, u32[]{:S(2)}, u32[]{:S(2)}) collective-permute-start(bf16[256,1024]{1,0:T(8,128)(2,1)} %collective-permute-done.9), channel_id=1, source_target_pairs={{0,15},{1,0},{2,1},{3,2},{4,3},{5,4},{6,5},{7,6},{8,7},{9,8},{10,9... | collective-permute-start | bytes 1572872 | tf_op jit(solution)/shard_map/ppermute | solution.py:28
  97.8 13.1 %collective-permute-start.12 = (bf16[256,1024]{1,0:T(8,128)(2,1)}, bf16[256,1024]{1,0:T(8,128)(2,1)S(1)}, u32[]{:S(2)}, u32[]{:S(2)}) collective-permute-start(bf16[256,1024]{1,0:T(8,128)(2,1)} %collective-permute-done.10), channel_id=1, source_target_pairs={{0,1},{1,2},{2,3},{3,4},{4,5},{5,6},{6,7},{7,8},{8,9},{9,10},{10,1... | collective-permute-start | bytes 1572872 | tf_op jit(solution)/shard_map/ppermute | solution.py:23
  98.7 25.6 %slice-start = ((bf16[1024,1,192]{0,2,1:T(8,128)(2,1)}), bf16[1024,1,128]{0,2,1:T(8,128)(2,1)S(1)}, s32[]{:S(2)}) async-start(bf16[1024,1,192]{0,2,1:T(8,128)(2,1)} %param.15), calls=%async_computation.1 | async-start | bytes 524288 | tf_op jit(solution)/shard_map/slice | solution.py:65
  98.7 25.6 %slice-start.1 = ((bf16[1024,1,192]{0,2,1:T(8,128)(2,1)}), bf16[1024,1,64]{0,2,1:T(8,128)(2,1)S(1)}, s32[]{:S(2)}) async-start(bf16[1024,1,192]{0,2,1:T(8,128)(2,1)} %param.15), calls=%async_computation.2 | async-start | bytes 262144 | tf_op jit(solution)/shard_map/slice | solution.py:65
  102.2 14.1 %collective-permute-start.13 = (bf16[256,1024]{1,0:T(8,128)(2,1)S(1)}, bf16[256,1024]{1,0:T(8,128)(2,1)S(1)}, u32[]{:S(2)}, u32[]{:S(2)}) collective-permute-start(bf16[256,1024]{1,0:T(8,128)(2,1)S(1)} %collective-permute-done.11), channel_id=1, source_target_pairs={{0,15},{1,0},{2,1},{3,2},{4,3},{5,4},{6,5},{7,6},{8,7},{9,8},{10,9... | collective-permute-start | bytes 1572872 | tf_op jit(solution)/shard_map/ppermute | solution.py:28
  110.9 12.5 %collective-permute-start.14 = (bf16[256,1024]{1,0:T(8,128)(2,1)S(1)}, bf16[256,1024]{1,0:T(8,128)(2,1)S(1)}, u32[]{:S(2)}, u32[]{:S(2)}) collective-permute-start(bf16[256,1024]{1,0:T(8,128)(2,1)S(1)} %collective-permute-done.12), channel_id=1, source_target_pairs={{0,1},{1,2},{2,3},{3,4},{4,5},{5,6},{6,7},{7,8},{8,9},{9,10},{10,1... | collective-permute-start | bytes 1572872 | tf_op jit(solution)/shard_map/ppermute | solution.py:23
  134.4 84.1 %copy-start.19 = (s32[32,8]{0,1:T(8,128)S(1)}, s32[32,8]{0,1:T(8,128)}, u32[]{:S(2)}) copy-start(s32[32,8]{0,1:T(8,128)} %param.20) | copy-start | bytes 3076
  152.7 19.1 %collective-permute-start.15 = (bf16[4096,128]{1,0:T(8,128)(2,1)S(1)}, bf16[4096,128]{1,0:T(8,128)(2,1)S(1)}, u32[]{:S(2)}, u32[]{:S(2)}) collective-permute-start(bf16[4096,128]{1,0:T(8,128)(2,1)S(1)} %broadcast_select_fusion.3), channel_id=1, source_target_pairs={{0,224},{16,240},{32,0},{48,16},{64,32},{80,48},{96,64},{112,80},{... | collective-permute-start | bytes 3145736 | tf_op jit(solution)/shard_map/ppermute | solution.py:37
  172.8 14.2 %collective-permute-start.16 = (bf16[4096,128]{1,0:T(8,128)(2,1)S(1)}, bf16[4096,128]{1,0:T(8,128)(2,1)S(1)}, u32[]{:S(2)}, u32[]{:S(2)}) collective-permute-start(bf16[4096,128]{1,0:T(8,128)(2,1)S(1)} %collective-permute-done.15), channel_id=1, source_target_pairs={{0,16},{16,32},{32,48},{48,64},{64,80},{80,96},{96,112},{112,128},... | collective-permute-start | bytes 3145736 | tf_op jit(solution)/shard_map/ppermute | solution.py:37
  188.0 14.2 %collective-permute-start.17 = (bf16[4096,128]{1,0:T(8,128)(2,1)S(1)}, bf16[4096,128]{1,0:T(8,128)(2,1)S(1)}, u32[]{:S(2)}, u32[]{:S(2)}) collective-permute-start(bf16[4096,128]{1,0:T(8,128)(2,1)S(1)} %collective-permute-done.16), channel_id=1, source_target_pairs={{0,16},{16,32},{32,48},{48,64},{64,80},{80,96},{96,112},{112,128},... | collective-permute-start | bytes 3145736 | tf_op jit(solution)/shard_map/ppermute | solution.py:37
  202.2 20.2 %copy-start.9 = (bf16[4096,128]{1,0:T(8,128)(2,1)}, bf16[4096,128]{1,0:T(8,128)(2,1)S(1)}, u32[]{:S(2)}) copy-start(bf16[4096,128]{1,0:T(8,128)(2,1)S(1)} %collective-permute-done.17) | copy-start | bytes 3145732
  202.2 16.5 %collective-permute-start.18 = (bf16[4096,128]{1,0:T(8,128)(2,1)S(1)}, bf16[4096,128]{1,0:T(8,128)(2,1)}, u32[]{:S(2)}, u32[]{:S(2)}) collective-permute-start(bf16[4096,128]{1,0:T(8,128)(2,1)S(1)} %collective-permute-done.17), channel_id=1, source_target_pairs={{0,16},{16,32},{32,48},{48,64},{64,80},{80,96},{96,112},{112,128},... | collective-permute-start | bytes 3145736 | tf_op jit(solution)/shard_map/ppermute | solution.py:37
  218.7 26.5 %collective-permute-start.19 = (bf16[4096,128]{1,0:T(8,128)(2,1)}, bf16[4096,128]{1,0:T(8,128)(2,1)}, u32[]{:S(2)}, u32[]{:S(2)}) collective-permute-start(bf16[4096,128]{1,0:T(8,128)(2,1)} %collective-permute-done.18), channel_id=1, source_target_pairs={{0,16},{16,32},{32,48},{48,64},{64,80},{80,96},{96,112},{112,128},... | collective-permute-start | bytes 3145736 | tf_op jit(solution)/shard_map/ppermute | solution.py:37
  369.3 22.2 %copy-start.20 = (f32[1024]{0:T(1024)S(1)}, f32[1024]{0:T(1024)}, u32[]{:S(2)}) copy-start(f32[1024]{0:T(1024)} %param.17) | copy-start | bytes 12292
  (11 other events, 44.1 us)
